TPU v7x, 32 devices: a whole 2x2x4 slice. The times are simulated.
32 devices in a mesh: blk: 8 (over z, x), rep: 4 (over y, core).
Axes of the slice: x: 2, y: 2, z: 4, core: 2. Of those that a mesh axis runs over, the one named last changes fastest.
Arguments:
- features: bfloat16 [32768, 128], P('blk'), may hold values from -6 to 6
- weight: bfloat16 [128, 256], replicated, may hold values from -0.5 to 0.5
- bias: float32 [256], replicated, may hold values from -3 to 3
- tile_values: bfloat16 [8, 8, 160, 128, 128], P('blk', 'rep'), may hold values from 0 to 0.041748047
- tile_place: int32 [8, 8, 160], P('blk', 'rep'), may hold values from 0 to 1023, as said below
- tile_count: int32 [8, 8], P('blk', 'rep'), may hold values from 1 to 160, as said below
Outputs:
- activations: bfloat16 [32768, 256], P('blk')
Inputs may be any that keep to these rules, and one draw needn't show every extreme that they name: `tile_place`: within one pair of destination block and section the 160 positions are distinct. `tile_count`: some pair of destination block and section has all 160 slots occupied.
All inputs are finite; a program needn't handle non-finite values.
Results may differ from a plain program's by a relative error of at most 0.0046.
Values may be sent and summed in bfloat16 or wider, within the bound.
A program may use at most 128 MiB of HBM per device.

v0:
```python
import functools
import heapq
import random

import jax
import jax.numpy as jnp
from jax import lax
from jax.experimental import pallas as pl
from jax.experimental.pallas import tpu as pltpu
from jax.sharding import PartitionSpec as P

MESH = pl.DeviceIdType.MESH
GROUP = 80
CHUNKS = 4
PIECES = 16
HOP = 6
WAIT = 7
ROUNDS = 40
LEAD = 0
PASSES = 768
SEED = 63485
EXPRESS = 1
URGENCY = 0.1
TOLL = 1.0
OUT_STEPS = 8
SWAPS = 8
GRANT = 16 * 1024 * 1024


def largest_divisor(number, most):
    return max(d for d in range(1, most + 1) if number % d == 0)


def chip_grid(blocks, replicas):
    columns = 2
    floors, planes = blocks // columns, replicas // 2
    chips = [(z, x, y) for z in range(floors) for x in range(columns) for y in range(planes)]
    ways = {}
    for z, x, y in chips:
        out = [(0, (z, columns - 1 - x, y), [(z, x, y, 0)])]
        out += [(3, (z, x, 1 - y), [(z, x, y, 3)])] if planes == 2 else [
            (3 + (side < 0), (z, x, y + side), [(z, x, y, 3 + (side < 0))])
            for side in (1, -1) if 0 <= y + side < planes]
        for far in range(1, EXPRESS + 1):
            for side in (1, -1):
                if 0 <= z + side * far < floors:
                    first = 1 if far == 1 else 2 * far + 1
                    crossed = [(z + side * k, x, y, 1 + (side < 0)) for k in range(far)]
                    out.append((first + (side < 0), (z + side * far, x, y), crossed))
        ways[z, x, y] = out
    return columns, planes, chips, ways


def plan_trees(blocks, replicas, sections, pieces, hop, passes):
    columns, planes, chips, ways = chip_grid(blocks, replicas)
    order = {chip: i for i, chip in enumerate(chips)}
    core_of = {}
    for b in range(blocks):
        for r in range(replicas):
            for i in range(sections):
                core_of[(b // columns, b % columns, r // 2), (b - r * sections - i) % blocks] = r % 2
    roots = {s: [(s // columns, s % columns, y) for y in range(planes)] for s in range(blocks)}
    wants = {s: [c for c in chips if (c, s) in core_of and c not in roots[s]] for s in range(blocks)}
    busy = {link: 0 for chip in chips for _, _, crossed in ways[chip] for link in crossed}
    load = dict.fromkeys(busy, 0)
    past = dict.fromkeys(busy, 0.0)
    trees, best = {}, None
    keys = [(s, p) for p in range(pieces) for s in range(blocks)]
    turn, draw = list(keys), SEED

    def grow(s, price):
        ready = dict.fromkeys(roots[s], 0)
        left, tree = set(wants[s]), []
        while left:
            cost, came, done = {}, {}, set()
            heap = [(URGENCY * t, t, order[c], c) for c, t in ready.items()]
            heapq.heapify(heap)
            while True:
                c, t, _, chip = heapq.heappop(heap)
                if chip in done:
                    continue
                done.add(chip)
                if chip in left:
                    break
                for way, other, crossed in ways[chip]:
                    if other in ready or other in done:
                        continue
                    taken, toll = 0, 0.0
                    for link in crossed:
                        taken |= busy[link]
                        toll += price[link]
                    taken >>= t
                    start = t + (~taken & (taken + 1)).bit_length() - 1
                    there = start + hop + len(crossed) - 1
                    total = c + URGENCY * (there - t) + toll
                    if other not in cost or total < cost[other]:
                        cost[other] = total
                        came[other] = (chip, way, start, crossed, there)
                        heapq.heappush(heap, (total, there, order[other], other))
            path = []
            while chip not in ready:
                path.append(came[chip] + (chip,))
                chip = came[chip][0]
            for chip, way, start, crossed, there, other in reversed(path):
                ready[other] = there
                for link in crossed:
                    busy[link] |= 1 << start
                    load[link] += 1
                tree.append((chip, way, start, other, crossed))
                left.discard(other)
        return tree

    for _ in range(passes):
        for key in turn:
            for _, _, start, _, crossed in trees.get(key, ()):
                for link in crossed:
                    busy[link] &= ~(1 << start)
                    load[link] -= 1
            top = max(max(load.values()), 1)
            trees[key] = grow(key[0], {k: TOLL * (past[k] + (load[k] / top) ** 4) for k in load})
        last = {key: max(start for _, _, start, _, _ in tree) for key, tree in trees.items()}
        span = max(last.values())
        score = (span, sum(v >= span - 1 for v in last.values()), sum(load.values()))
        if best is None or score < best[0]:
            best = (score, {key: list(tree) for key, tree in trees.items()})
        top = max(load.values())
        for k in load:
            past[k] = past[k] * 0.9 + (0.2 if load[k] >= top - pieces * 0.05 else 0.0)
        ranks = []
        for key in keys:
            draw = (draw * 1103515245 + 12345) % (1 << 31)
            ranks.append(((draw >> 8) % 1000 / 125 - last[key], key))
        turn = [key for _, key in sorted(ranks)]
    return best[1], core_of


def list_times(trees, hop, bonus):
    kids, to_go, queues, arrivals = {}, {}, {}, {}
    starts, last, number, slot = {}, dict.fromkeys(trees, 0), 0, 0
    left = sum(len(tree) for tree in trees.values())

    def enqueue(key, i):
        nonlocal number
        chip, way = trees[key][i][:2]
        heapq.heappush(queues.setdefault((chip, way), []), (-(to_go[key][i] * hop + bonus[key]), number, key, i))
        number += 1

    for key, tree in trees.items():
        kids[key], to_go[key] = {}, {}
        for i, (chip, _, _, _, _) in enumerate(tree):
            kids[key].setdefault(chip, []).append(i)
        for i in reversed(range(len(tree))):
            to_go[key][i] = 1 + max([to_go[key][j] for j in kids[key].get(tree[i][3], [])], default=0)
        reached = {other for _, _, _, other, _ in tree}
        for i, (chip, _, _, _, _) in enumerate(tree):
            if chip not in reached:
                enqueue(key, i)
    while left:
        for key, i in arrivals.pop(slot, []):
            for j in kids[key].get(trees[key][i][3], []):
                enqueue(key, j)
        for queue in queues.values():
            if queue:
                _, _, key, i = heapq.heappop(queue)
                starts[key, i] = slot
                arrivals.setdefault(slot + hop, []).append((key, i))
                last[key] = max(last[key], slot + hop)
                left -= 1
        slot += 1
    return starts, last


def retime(trees, hop, rounds):
    draw, bonus, best = random.Random(1), dict.fromkeys(trees, 0.0), None
    for _ in range(rounds):
        starts, last = list_times(trees, hop, bonus)
        span = max(last.values())
        score = (span, sum(v >= span - 1 for v in last.values()))
        if best is None or score < best[0]:
            best = (score, starts)
        for key in bonus:
            late = 1.0 if last[key] >= span - 1 else 0.3 if last[key] >= span - 3 else 0.0
            bonus[key] = bonus[key] * 0.95 + late * draw.random() * 2
    return {
        key: [(chip, way, best[1][key, i], other, crossed) for i, (chip, way, _, other, crossed) in enumerate(tree)]
        for key, tree in trees.items()}


def plan_gather(blocks, replicas, sections, pieces, hop, passes):
    trees, core_of = plan_trees(blocks, replicas, sections, pieces, hop, passes)
    trees = retime(trees, WAIT, ROUNDS)
    columns, planes, chips, _ = chip_grid(blocks, replicas)
    devices = blocks * replicas
    actions = [[] for _ in range(devices)]
    arrived = [set() for _ in range(devices)]

    def core(chip, s, p):
        return core_of.get((chip, s), p % 2) if chip[:2] != (s // columns, s % columns) else p % 2

    def device(chip, c):
        return (chip[0] * columns + chip[1]) * replicas + chip[2] * 2 + c

    for (s, p), tree in sorted(trees.items()):
        for chip, way, start, other, _ in tree:
            here, there = core(chip, s, p), core(other, s, p)
            own = chip[:2] == (s // columns, s % columns)
            actions[device(chip, here)].append((start - (LEAD if own else 0), not own, s * pieces + p, way, there))
            arrived[device(other, there)].add(s * pieces + p)
    plans = []
    for d in range(devices):
        slots, waited = [], set()
        for _, relay, piece, way, there in sorted(actions[d]):
            spot = None
            for j in range(len(slots) - 1, -1, -1):
                if slots[j][0] == piece:
                    spot = j
                    break
                if way in slots[j][2]:
                    break
            if spot is None:
                slots.append((piece, relay and piece not in waited, {}))
                spot = len(slots) - 1
                if relay:
                    waited.add(piece)
            slots[spot][2][way] = there
        leaves = arrived[d] - waited
        plans.append((slots, leaves))
    return plans


def used_ways(plans):
    used = {way for slots, _ in plans for _, _, sends in slots for way in sends}
    pairs = {1: 2, 2: 1, 3: 3, 4: 3}
    return sorted(used | {0 if w == 0 else pairs.get(w, w + 1 if w % 2 else w - 1) for w in used})


def gather_kernel(blocks, replicas, sections, pieces, plans, features_ref, tiles_ref, all_ref, held_ref,
                  table_ref, recv_sem, send_sem, own_sem, held_sem):
    blk, rep = lax.axis_index("blk"), lax.axis_index("rep")
    columns, planes, _, _ = chip_grid(blocks, replicas)
    floors = blocks // columns
    rows = features_ref.shape[0]
    size = rows // pieces
    z, x = lax.div(blk, columns), lax.rem(blk, columns)
    y, me = lax.div(rep, 2), lax.rem(rep, 2)
    is_blk = [blk == b for b in range(blocks)]
    is_rep = [rep == r for r in range(replicas)]

    def choose(options, tests):
        value = jnp.int32(options[0])
        for option, test in zip(options[1:], tests[1:]):
            value = jnp.where(test, option, value)
        return value

    def pick(values):
        if len(set(values)) == 1:
            return jnp.int32(values[0])
        picked = []
        for b in range(blocks):
            row = values[b * replicas:(b + 1) * replicas]
            picked.append(row[0] if len(set(row)) == 1 else choose(row, is_rep))
        return choose(picked, is_blk)

    def target(way, c):
        if way == 0:
            return (z * columns + (columns - 1 - x), y * 2 + c)
        if way in (3, 4):
            return (blk, (1 - y if planes == 2 else y + (1 if way == 3 else -1)) * 2 + c)
        far = 1 if way < 3 else (way - 1) // 2
        return (blk + (far if way % 2 else -far) * columns, y * 2 + c)

    exists = {}
    for way in used_ways(plans):
        if way == 0 or (way == 3 and planes == 2):
            exists[way] = None
        elif way in (3, 4):
            exists[way] = y < planes - 1 if way == 3 else y > 0
        else:
            far = 1 if way < 3 else (way - 1) // 2
            exists[way] = z < floors - far if way % 2 else z >= far

    own = pltpu.make_async_copy(features_ref, all_ref.at[blk], own_sem)
    own.start()
    steps = max(len(slots) for slots, _ in plans)
    ways = sorted(exists)
    shift = pieces.bit_length() - 1
    for j in range(steps):
        values = []
        for slots, _ in plans:
            piece, relay, sends = slots[j] if j < len(slots) else (0, False, {})
            values.append((piece * 2 + int(relay) << 2 * len(ways)) + sum(2 + sends[w] << 2 * k for k, w in enumerate(ways) if w in sends))
        table_ref[j] = pick(values)
    run = min(pieces, 16)
    words = [(i, first) for i in range(sections) for first in range(0, pieces, run)]
    for n, (i, first) in enumerate(words):
        values = []
        for d, (_, leaves) in enumerate(plans):
            s = (d // replicas - d % replicas * sections - i) % blocks
            values.append(sum(1 << p for p in range(run) if s * pieces + first + p in leaves))
        table_ref[steps + n] = pick(values)

    barrier = pltpu.get_barrier_semaphore()
    count = jnp.int32(0)
    for way, test in exists.items():
        def greet(way=way):
            for c in range(2):
                pl.semaphore_signal(barrier, inc=1, device_id=target(way, c), device_id_type=MESH)
        if test is None:
            greet()
            count = count + 2
        else:
            pl.when(test)(greet)
            count = count + jnp.where(test, 2, 0)
    pl.semaphore_wait(barrier, count)

    def block(piece):
        return all_ref.at[piece >> shift, pl.ds(pl.multiple_of((piece & (pieces - 1)) * size, size), size)]

    def copy(piece, way, c, j):
        return pltpu.make_async_remote_copy(
            src_ref=block(piece), dst_ref=block(piece), send_sem=send_sem.at[j, ways.index(way)],
            recv_sem=recv_sem.at[piece], device_id=target(way, c), device_id_type=MESH)

    def unpack(j):
        value = table_ref[j]
        return value >> (2 * len(ways) + 1), (value >> (2 * len(ways))) & 1 == 1, [
            (way, (value >> (2 * k + 1)) & 1 == 1, (value >> (2 * k)) & 1) for k, way in enumerate(ways)]

    own.wait()
    held = pltpu.make_async_copy(tiles_ref, held_ref, held_sem)
    held.start()

    def step(j, carry):
        piece, relay, sends = unpack(j)
        pl.when(relay)(lambda: copy(piece, 0, 0, j).wait_recv())
        for way, test, c in sends:
            pl.when(test)(lambda way=way, c=c: copy(piece, way, c, j).start())
        return carry

    def drain(j, carry):
        piece, _, sends = unpack(j)
        for way, test, c in sends:
            pl.when(test)(lambda way=way, c=c: copy(piece, way, c, j).wait_send())
        return carry

    lax.fori_loop(0, steps, step, 0)
    lax.fori_loop(0, steps * 3 // 4, drain, 0)
    for n, (i, first) in enumerate(words):
        source = lax.rem(blk - rep * sections - i + blocks, blocks)
        mask = table_ref[steps + n]

        def leaf(p, carry, start=source * pieces + first, mask=mask):
            pl.when((mask >> p) & 1 == 1)(lambda: copy(start + p, 0, 0, 0).wait_recv())
            return carry

        lax.fori_loop(0, run, leaf, 0)
    lax.fori_loop(steps * 3 // 4, steps, drain, 0)
    held.wait()


def gather_sources(features, tile_values, blocks, replicas):
    sections = tile_values.shape[1]
    rows, width = features.shape
    pieces = PIECES
    while rows % (16 * pieces):
        pieces //= 2
    plans = plan_gather(blocks, replicas, sections, pieces, HOP, max(2, PASSES // (blocks * replicas)))
    steps = max(len(slots) for slots, _ in plans)
    ways = len(used_ways(plans))
    vmem = pl.BlockSpec(memory_space=pltpu.VMEM)
    hbm = pl.BlockSpec(memory_space=pltpu.HBM)
    dma = pltpu.SemaphoreType.DMA
    return pl.pallas_call(
        functools.partial(gather_kernel, blocks, replicas, sections, pieces, plans),
        out_shape=(
            jax.ShapeDtypeStruct((blocks, rows, width), features.dtype),
            jax.ShapeDtypeStruct(tile_values.shape, tile_values.dtype),
        ),
        in_specs=[hbm, hbm],
        out_specs=(vmem, vmem),
        scratch_shapes=[
            pltpu.SMEM((steps + sections * pl.cdiv(pieces, 16),), jnp.int32), dma((blocks * pieces,)), dma((steps, ways)), dma(()), dma(())
        ],
        compiler_params=pltpu.CompilerParams(collective_id=1, has_side_effects=True, vmem_limit_bytes=2 * GRANT),
        cost_estimate=pl.CostEstimate(
            flops=0, bytes_accessed=96 * rows * width * features.dtype.itemsize, transcendentals=0
        ),
        name="gather_sources",
    )(pltpu.with_memory_space_constraint(features, pltpu.HBM), tile_values)


def sections_kernel(group, place_ref, count_ref, source_ref, tiles_ref, acc_ref):
    sections, slots, tile = tiles_ref.shape[1:4]
    blocks, row_tiles = source_ref.shape[0], source_ref.shape[1] // tile
    blk, rep = lax.axis_index("blk"), lax.axis_index("rep")
    acc_ref[...] = jnp.zeros_like(acc_ref)
    for section in range(sections):
        source = lax.rem(blk - rep * sections - section + blocks, blocks)
        count = count_ref[0, section]

        def body(g, carry, section=section, source=source, count=count):
            for u in range(group):
                k = g * group + u
                place = place_ref[0, section, k]
                column, target = lax.rem(place, row_tiles), lax.div(place, row_tiles)
                piece = source_ref[source, pl.ds(pl.multiple_of(column * tile, tile), tile), :]
                product = jnp.dot(tiles_ref[0, section, k], piece, preferred_element_type=jnp.float32)
                rows = pl.ds(pl.multiple_of(target * tile, tile), tile)
                acc_ref[rows, :] += jnp.where(k < count, product, 0.0)
            return carry

        lax.fori_loop(0, lax.div(count + group - 1, group), body, 0)


def section_sums(sources, tile_values, tile_place, tile_count):
    slots = tile_values.shape[2]
    rows, width = sources.shape[1:]
    vmem = pl.BlockSpec(memory_space=pltpu.VMEM)
    smem = pl.BlockSpec(memory_space=pltpu.SMEM)
    return pl.pallas_call(
        functools.partial(sections_kernel, largest_divisor(slots, GROUP)),
        out_shape=jax.ShapeDtypeStruct((rows, width), jnp.float32),
        in_specs=[smem, smem, vmem, vmem],
        out_specs=vmem,
        compiler_params=pltpu.CompilerParams(vmem_limit_bytes=2 * GRANT),
        name="section_sums",
    )(tile_place, tile_count, sources, tile_values)


def swap_kernel(chunks, part_ref, agg_ref, core_in, send_buf, recv_buf, s1, r1, s2, r2, s3, r3):
    blk, rep = lax.axis_index("blk"), lax.axis_index("rep")
    core, chip = lax.rem(rep, 2), lax.div(rep, 2)
    half = part_ref.shape[0] // 2
    size = half // chunks
    other, across = chip * 2 + (1 - core), (1 - chip) * 2 + core

    def place(which, ch):
        return pl.ds(pl.multiple_of(which * half + ch * size, size), size)

    barrier = pltpu.get_barrier_semaphore()
    for target in (other, across):
        pl.semaphore_signal(barrier, inc=1, device_id=(blk, target), device_id_type=MESH)
    pl.semaphore_wait(barrier, 2)

    stage1, stage2, stage3 = [], [], []
    for ch in range(chunks):
        stage1.append(pltpu.make_async_remote_copy(
            src_ref=part_ref.at[place(1 - core, ch)], dst_ref=core_in.at[ch],
            send_sem=s1.at[ch], recv_sem=r1.at[ch], device_id=(blk, other), device_id_type=MESH))
        stage1[ch].start()
    for ch in range(chunks):
        stage1[ch].wait_recv()
        send_buf[ch] = (part_ref[place(core, ch), :] + core_in[ch]).astype(send_buf.dtype)
        stage2.append(pltpu.make_async_remote_copy(
            src_ref=send_buf.at[ch], dst_ref=recv_buf.at[ch],
            send_sem=s2.at[ch], recv_sem=r2.at[ch], device_id=(blk, across), device_id_type=MESH))
        stage2[ch].start()
    for ch in range(chunks):
        stage2[ch].wait_recv()
        mine = place(core, ch)
        total = send_buf[ch].astype(jnp.float32) + recv_buf[ch].astype(jnp.float32)
        agg_ref[mine, :] = total.astype(agg_ref.dtype)
        stage3.append(pltpu.make_async_remote_copy(
            src_ref=agg_ref.at[mine], dst_ref=agg_ref.at[mine],
            send_sem=s3.at[ch], recv_sem=r3.at[ch], device_id=(blk, other), device_id_type=MESH))
        stage3[ch].start()
    for ch in range(chunks):
        stage1[ch].wait_send()
        stage2[ch].wait_send()
        stage3[ch].wait()


def pair_sum(part):
    rows, width = part.shape
    chunks = largest_divisor(rows // 2 // 16, SWAPS)
    size = rows // 2 // chunks
    dma = pltpu.SemaphoreType.DMA((chunks,))
    vmem = pl.BlockSpec(memory_space=pltpu.VMEM)
    return pl.pallas_call(
        functools.partial(swap_kernel, chunks),
        out_shape=jax.ShapeDtypeStruct((rows, width), jnp.bfloat16),
        in_specs=[vmem],
        out_specs=vmem,
        scratch_shapes=[
            pltpu.VMEM((chunks, size, width), jnp.float32),
            pltpu.VMEM((chunks, size, width), jnp.bfloat16),
            pltpu.VMEM((chunks, size, width), jnp.bfloat16),
        ] + [dma] * 6,
        compiler_params=pltpu.CompilerParams(collective_id=0, has_side_effects=True, vmem_limit_bytes=GRANT),
        name="replica_sum",
    )(part)


def reduce_kernel(chips, chunks, part_ref, agg_ref, core_in, send_buf, recv_buf,
                  s1, r1, s2, r2, s3, r3, s4, r4):
    blk, rep = lax.axis_index("blk"), lax.axis_index("rep")
    core, chip = lax.rem(rep, 2), lax.div(rep, 2)
    rows = part_ref.shape[0]
    half = rows // 2
    size = half // chips // chunks
    other = chip * 2 + (1 - core)

    def peer(d):
        return lax.rem(chip + d, chips)

    def local(piece, ch):
        return pl.ds(pl.multiple_of((piece * chunks + ch) * size, size), size)

    def place(which, piece, ch):
        return pl.ds(pl.multiple_of(which * half + (piece * chunks + ch) * size, size), size)

    barrier = pltpu.get_barrier_semaphore()
    pl.semaphore_signal(barrier, inc=1, device_id=(blk, other), device_id_type=MESH)
    for d in range(1, chips):
        pl.semaphore_signal(barrier, inc=1, device_id=(blk, peer(d) * 2 + core), device_id_type=MESH)
    pl.semaphore_wait(barrier, chips)

    order = [(ch, d) for ch in range(chunks) for d in list(range(1, chips)) + [0]]
    stage1, stage2, stage3, stage4 = {}, {}, {}, {}
    for ch, d in order:
        copy = pltpu.make_async_remote_copy(
            src_ref=part_ref.at[place(1 - core, peer(d), ch)], dst_ref=core_in.at[local(peer(d), ch)],
            send_sem=s1.at[d, ch], recv_sem=r1.at[d, ch], device_id=(blk, other), device_id_type=MESH)
        copy.start()
        stage1[ch, d] = copy
    for ch, d in order:
        if d == 0:
            continue
        stage1[ch, d].wait_recv()
        total = part_ref[place(core, peer(d), ch), :] + core_in[local(peer(d), ch), :]
        send_buf[d - 1, ch] = total.astype(jnp.bfloat16)
        copy = pltpu.make_async_remote_copy(
            src_ref=send_buf.at[d - 1, ch], dst_ref=recv_buf.at[d - 1, ch],
            send_sem=s2.at[d, ch], recv_sem=r2.at[d, ch],
            device_id=(blk, peer(d) * 2 + core), device_id_type=MESH)
        copy.start()
        stage2[ch, d] = copy
    for ch in range(chunks):
        stage1[ch, 0].wait_recv()
        total = part_ref[place(core, chip, ch), :] + core_in[local(chip, ch), :]
        for d in range(1, chips):
            stage2[ch, d].wait_recv()
            total = total + recv_buf[d - 1, ch].astype(jnp.float32)
        mine = place(core, chip, ch)
        agg_ref[mine, :] = total.astype(jnp.bfloat16)
        for d in list(range(1, chips)) + [0]:
            target = other if d == 0 else peer(d) * 2 + core
            copy = pltpu.make_async_remote_copy(
                src_ref=agg_ref.at[mine], dst_ref=agg_ref.at[mine],
                send_sem=s3.at[d, ch], recv_sem=r3.at[d, ch],
                device_id=(blk, target), device_id_type=MESH)
            copy.start()
            stage3[ch, d] = copy
    for ch in range(chunks):
        for d in range(1, chips):
            stage3[ch, d].wait_recv()
            came = place(core, lax.rem(chip + chips - d, chips), ch)
            copy = pltpu.make_async_remote_copy(
                src_ref=agg_ref.at[came], dst_ref=agg_ref.at[came],
                send_sem=s4.at[d, ch], recv_sem=r4.at[d, ch],
                device_id=(blk, other), device_id_type=MESH)
            copy.start()
            stage4[ch, d] = copy
    for ch, d in order:
        stage1[ch, d].wait_send()
        stage3[ch, d].wait_send()
        if d == 0:
            stage3[ch, d].wait_recv()
        else:
            stage2[ch, d].wait_send()
            stage4[ch, d].wait()


def replica_sum(part, replicas):
    rows, width = part.shape
    chips = replicas // 2
    chunks = largest_divisor(rows // 2 // chips // 16, CHUNKS)
    size = rows // 2 // chips // chunks
    dma = pltpu.SemaphoreType.DMA((chips, chunks))
    vmem = pl.BlockSpec(memory_space=pltpu.VMEM)
    return pl.pallas_call(
        functools.partial(reduce_kernel, chips, chunks),
        out_shape=jax.ShapeDtypeStruct((rows, width), jnp.bfloat16),
        in_specs=[vmem],
        out_specs=vmem,
        scratch_shapes=[
            pltpu.VMEM((rows // 2, width), jnp.float32),
            pltpu.VMEM((chips - 1, chunks, size, width), jnp.bfloat16),
            pltpu.VMEM((chips - 1, chunks, size, width), jnp.bfloat16),
        ] + [dma] * 8,
        compiler_params=pltpu.CompilerParams(collective_id=0, has_side_effects=True, vmem_limit_bytes=GRANT),
        name="replica_sum",
    )(part)


def activate_kernel(steps, agg_ref, weight_ref, bias_ref, out_ref, buffer, sems):
    size = agg_ref.shape[0] // steps
    copies = []
    for i in range(steps):
        span = pl.ds(i * size, size)
        output = jnp.dot(agg_ref[span, :], weight_ref[...], preferred_element_type=jnp.float32) + bias_ref[...]
        buffer[span, :] = jnp.maximum(output, 0.0).astype(buffer.dtype)
        copies.append(pltpu.make_async_copy(buffer.at[span], out_ref.at[span], sems.at[i]))
        copies[i].start()
    for copy in copies:
        copy.wait()


def activate(aggregated, weight, bias):
    rows, width = aggregated.shape
    hidden = weight.shape[1]
    steps = largest_divisor(rows // 16, OUT_STEPS)
    vmem = pl.BlockSpec(memory_space=pltpu.VMEM)
    return pl.pallas_call(
        functools.partial(activate_kernel, steps),
        out_shape=jax.ShapeDtypeStruct((rows, hidden), jnp.bfloat16),
        in_specs=[vmem, vmem, vmem],
        out_specs=pl.BlockSpec(memory_space=pltpu.HBM),
        scratch_shapes=[pltpu.VMEM((rows, hidden), jnp.bfloat16), pltpu.SemaphoreType.DMA((steps,))],
        compiler_params=pltpu.CompilerParams(vmem_limit_bytes=GRANT),
        name="activate",
    )(aggregated, weight, bias[None, :])


def shards(blocks, replicas, features, weight, bias, tile_values, tile_place, tile_count):
    sources, held = gather_sources(features, tile_values, blocks, replicas)
    part = section_sums(sources, held, tile_place, tile_count)
    aggregated = pair_sum(part) if replicas == 4 else replica_sum(part, replicas)
    return activate(aggregated, weight, bias)


def solution(mesh):
    in_specs = (
        P("blk", None),
        P(),
        P(),
        P("blk", "rep", None, None, None),
        P("blk", "rep", None),
        P("blk", "rep"),
    )
    body = functools.partial(shards, mesh.shape["blk"], mesh.shape["rep"])
    return jax.shard_map(body, mesh=mesh, in_specs=in_specs, out_specs=P("blk", None), check_vma=False)
```

profile of v0, /device:TPU:0, one launch (start us, length us, event | category | flops | bytes accessed | tf_op | source)
XLA Modules:
  0.0 54.0 jit_solution(15341535761850755840)
XLA Ops:
  0.0 0.0 copy-start.3
  0.0 0.0 copy-start.1
  0.0 32.0 %gather_sources.1 = (bf16[8,4096,128]{2,1,0:T(8,128)(2,1)S(1)}, bf16[1,2,160,128,128]{4,3,2,1,0:T(8,128)(2,1)S(1)}) custom-call(bf16[4096,128]{1,0:T(8,128)(2,1)} %features_ref.1, bf16[1,2,160,128,128]{4,3,2,1,0:T(8,128)(2,1)} %tiles_ref.1), custom_call_target="tpu_custom_call" | custom-call | bytes 100663296 | tf_op jit(solution)/shard_map/gather_sources/pallas_call | solution.py:373
  32.0 0.0 copy-done.3
  32.1 0.0 copy-done.1
  32.1 0.0 copy-start
  32.1 0.0 copy-start.2
  32.1 3.7 %section_sums.1.part_ref = f32[4096,128]{1,0:T(8,128)S(1)} custom-call(s32[1,2,160]{2,1,0:T(2,128)S(1)} %copy-done.1, s32[1,2]{1,0:T(1,128)S(1)} %copy-done.3, bf16[8,4096,128]{2,1,0:T(8,128)(2,1)S(1)} %get-tuple-element.7.source_ref, bf16[1,2,160,128,128]{4,3,2,1,0:T(8,128)(2,1)S(1)} %get-tuple-element.8.tiles_ref), custom_call_target="tpu_custom_call" | custom-call | tf_op jit(solution)/shard_map/section_sums/pallas_call | solution.py:420
  35.7 16.5 %replica_sum.1.agg_ref = bf16[4096,128]{1,0:T(8,128)(2,1)S(1)} custom-call(f32[4096,128]{1,0:T(8,128)S(1)} %section_sums.1.part_ref), custom_call_target="tpu_custom_call" | custom-call | tf_op jit(solution)/shard_map/replica_sum/pallas_call | solution.py:479
  52.3 0.0 copy-done
  52.3 0.0 copy-done.2
  52.3 1.7 %activate.1 = bf16[4096,256]{1,0:T(8,128)(2,1)} custom-call(bf16[4096,128]{1,0:T(8,128)(2,1)S(1)} %replica_sum.1.agg_ref, bf16[128,256]{1,0:T(8,128)(2,1)S(1)} %copy-done, f32[1,256]{1,0:T(1,128)S(1)} %bitcast.1), custom_call_target="tpu_custom_call" | custom-call | tf_op jit(solution)/shard_map/activate/pallas_call | solution.py:614
Async XLA Ops:
  0.0 32.0 %copy-start.3 = (s32[1,2]{1,0:T(1,128)S(1)}, s32[1,2]{1,0:T(1,128)}, u32[]{:S(2)}) copy-start(s32[1,2]{1,0:T(1,128)} %count_ref.1) | copy-start | bytes 28
  0.0 32.1 %copy-start.1 = (s32[1,2,160]{2,1,0:T(2,128)S(1)}, s32[1,2,160]{2,1,0:T(2,128)}, u32[]{:S(2)}) copy-start(s32[1,2,160]{2,1,0:T(2,128)} %place_ref.1) | copy-start | bytes 3844
  32.1 20.2 %copy-start = (bf16[128,256]{1,0:T(8,128)(2,1)S(1)}, bf16[128,256]{1,0:T(8,128)(2,1)}, u32[]{:S(2)}) copy-start(bf16[128,256]{1,0:T(8,128)(2,1)} %weight_ref.1) | copy-start | bytes 196612
  32.1 20.2 %copy-start.2 = (f32[256]{0:T(256)S(1)}, f32[256]{0:T(256)}, u32[]{:S(2)}) copy-start(f32[256]{0:T(256)} %param.8) | copy-start | bytes 3076
where the time goes:
time: 54.1 us; the launch traced here: 54 us
  Pallas kernels  53.9 us (100%)
    pallas_call x1, Pallas kernels, gather_sources(): pl.pallas_call(functools.partial(gather_kernel, blocks, replicas, section...  32 us
    pallas_call x1, Pallas kernels, pair_sum(): pl.pallas_call(functools.partial(swap_kernel, chunks), out_shape=jax.Shap...  16.5 us
    pallas_call x1, Pallas kernels, section_sums(): pl.pallas_call(functools.partial(sections_kernel, largest_divisor(slots,...  3.66 us
    pallas_call x1, Pallas kernels, activate(): pl.pallas_call(functools.partial(activate_kernel, steps), out_shape=jax.S...  1.66 us

commit v1 on v0

--- a/solution.py
+++ b/solution.py
@@ -23,7 +23,7 @@
 URGENCY = 0.1
 TOLL = 1.0
 OUT_STEPS = 8
-SWAPS = 8
+SWAPS = (1,) * 8
 GRANT = 16 * 1024 * 1024
 
 
@@ -281,6 +281,18 @@
 
     own = pltpu.make_async_copy(features_ref, all_ref.at[blk], own_sem)
     own.start()
+    barrier = pltpu.get_barrier_semaphore()
+    count = jnp.int32(0)
+    for way, test in exists.items():
+        def greet(way=way):
+            for c in range(2):
+                pl.semaphore_signal(barrier, inc=1, device_id=target(way, c), device_id_type=MESH)
+        if test is None:
+            greet()
+            count = count + 2
+        else:
+            pl.when(test)(greet)
+            count = count + jnp.where(test, 2, 0)
     steps = max(len(slots) for slots, _ in plans)
     ways = sorted(exists)
     shift = pieces.bit_length() - 1
@@ -298,19 +310,6 @@
             s = (d // replicas - d % replicas * sections - i) % blocks
             values.append(sum(1 << p for p in range(run) if s * pieces + first + p in leaves))
         table_ref[steps + n] = pick(values)
-
-    barrier = pltpu.get_barrier_semaphore()
-    count = jnp.int32(0)
-    for way, test in exists.items():
-        def greet(way=way):
-            for c in range(2):
-                pl.semaphore_signal(barrier, inc=1, device_id=target(way, c), device_id_type=MESH)
-        if test is None:
-            greet()
-            count = count + 2
-        else:
-            pl.when(test)(greet)
-            count = count + jnp.where(test, 2, 0)
     pl.semaphore_wait(barrier, count)
 
     def block(piece):
@@ -398,9 +397,9 @@
         source = lax.rem(blk - rep * sections - section + blocks, blocks)
         count = count_ref[0, section]
 
-        def body(g, carry, section=section, source=source, count=count):
-            for u in range(group):
-                k = g * group + u
+        def body(g, carry, size=group, first=0, section=section, source=source, count=count):
+            for u in range(size):
+                k = first + g * size + u
                 place = place_ref[0, section, k]
                 column, target = lax.rem(place, row_tiles), lax.div(place, row_tiles)
                 piece = source_ref[source, pl.ds(pl.multiple_of(column * tile, tile), tile), :]
@@ -409,7 +408,12 @@
                 acc_ref[rows, :] += jnp.where(k < count, product, 0.0)
             return carry
 
-        lax.fori_loop(0, lax.div(count + group - 1, group), body, 0)
+        half = group // 2 if group % 2 == 0 else group
+        full = lax.div(count + group - half - 1, group)
+        lax.fori_loop(0, full, body, 0)
+        if half < group:
+            left = count - full * group
+            lax.fori_loop(0, jnp.where(left > 0, 1, 0), functools.partial(body, size=half, first=full * group), 0)
 
 
 def section_sums(sources, tile_values, tile_place, tile_count):
@@ -427,15 +431,22 @@
     )(tile_place, tile_count, sources, tile_values)
 
 
-def swap_kernel(chunks, part_ref, agg_ref, core_in, send_buf, recv_buf, s1, r1, s2, r2, s3, r3):
+def swap_kernel(sizes, part_ref, weight_ref, bias_ref, act_ref, agg_ref, core_in, send_buf, recv_buf,
+                s1, r1, s2, r2, s3, r3):
     blk, rep = lax.axis_index("blk"), lax.axis_index("rep")
     core, chip = lax.rem(rep, 2), lax.div(rep, 2)
     half = part_ref.shape[0] // 2
-    size = half // chunks
     other, across = chip * 2 + (1 - core), (1 - chip) * 2 + core
+    chunks = len(sizes)
+    spans = [pl.ds(sum(sizes[:ch]), sizes[ch]) for ch in range(chunks)]
 
     def place(which, ch):
-        return pl.ds(pl.multiple_of(which * half + ch * size, size), size)
+        return pl.ds(pl.multiple_of(which * half + sum(sizes[:ch]), min(sizes)), sizes[ch])
+
+    def finish(which, ch):
+        span = place(which, ch)
+        output = jnp.dot(agg_ref[span, :], weight_ref[...], preferred_element_type=jnp.float32) + bias_ref[...]
+        act_ref[span, :] = jnp.maximum(output, 0.0).astype(act_ref.dtype)
 
     barrier = pltpu.get_barrier_semaphore()
     for target in (other, across):
@@ -443,52 +454,85 @@
     pl.semaphore_wait(barrier, 2)
 
     stage1, stage2, stage3 = [], [], []
-    for ch in range(chunks):
+    for ch, span in enumerate(spans):
         stage1.append(pltpu.make_async_remote_copy(
-            src_ref=part_ref.at[place(1 - core, ch)], dst_ref=core_in.at[ch],
+            src_ref=part_ref.at[place(1 - core, ch)], dst_ref=core_in.at[span],
             send_sem=s1.at[ch], recv_sem=r1.at[ch], device_id=(blk, other), device_id_type=MESH))
         stage1[ch].start()
-    for ch in range(chunks):
+    for ch, span in enumerate(spans):
         stage1[ch].wait_recv()
-        send_buf[ch] = (part_ref[place(core, ch), :] + core_in[ch]).astype(send_buf.dtype)
+        send_buf[span, :] = (part_ref[place(core, ch), :] + core_in[span, :]).astype(send_buf.dtype)
         stage2.append(pltpu.make_async_remote_copy(
-            src_ref=send_buf.at[ch], dst_ref=recv_buf.at[ch],
+            src_ref=send_buf.at[span], dst_ref=recv_buf.at[span],
             send_sem=s2.at[ch], recv_sem=r2.at[ch], device_id=(blk, across), device_id_type=MESH))
         stage2[ch].start()
-    for ch in range(chunks):
+    for ch, span in enumerate(spans):
         stage2[ch].wait_recv()
         mine = place(core, ch)
-        total = send_buf[ch].astype(jnp.float32) + recv_buf[ch].astype(jnp.float32)
+        total = send_buf[span, :].astype(jnp.float32) + recv_buf[span, :].astype(jnp.float32)
         agg_ref[mine, :] = total.astype(agg_ref.dtype)
         stage3.append(pltpu.make_async_remote_copy(
             src_ref=agg_ref.at[mine], dst_ref=agg_ref.at[mine],
             send_sem=s3.at[ch], recv_sem=r3.at[ch], device_id=(blk, other), device_id_type=MESH))
         stage3[ch].start()
+        finish(core, ch)
+        if ch:
+            stage3[ch - 1].wait_recv()
+            finish(1 - core, ch - 1)
     for ch in range(chunks):
         stage1[ch].wait_send()
         stage2[ch].wait_send()
-        stage3[ch].wait()
-
-
-def pair_sum(part):
+    stage3[chunks - 1].wait_recv()
+    finish(1 - core, chunks - 1)
+    for ch in range(chunks):
+        stage3[ch].wait_send()
+
+
+def swap_and_activate(part, weight, bias):
     rows, width = part.shape
-    chunks = largest_divisor(rows // 2 // 16, SWAPS)
-    size = rows // 2 // chunks
-    dma = pltpu.SemaphoreType.DMA((chunks,))
+    hidden = weight.shape[1]
+    half = rows // 2
+    unit = half // sum(SWAPS)
+    sizes = [unit * share for share in SWAPS] if unit * sum(SWAPS) == half and unit % 16 == 0 else [half]
+    dma = pltpu.SemaphoreType.DMA((len(sizes),))
     vmem = pl.BlockSpec(memory_space=pltpu.VMEM)
     return pl.pallas_call(
-        functools.partial(swap_kernel, chunks),
-        out_shape=jax.ShapeDtypeStruct((rows, width), jnp.bfloat16),
-        in_specs=[vmem],
+        functools.partial(swap_kernel, sizes),
+        out_shape=jax.ShapeDtypeStruct((rows, hidden), jnp.bfloat16),
+        in_specs=[vmem, vmem, vmem],
         out_specs=vmem,
         scratch_shapes=[
-            pltpu.VMEM((chunks, size, width), jnp.float32),
-            pltpu.VMEM((chunks, size, width), jnp.bfloat16),
-            pltpu.VMEM((chunks, size, width), jnp.bfloat16),
+            pltpu.VMEM((rows, width), jnp.bfloat16),
+            pltpu.VMEM((half, width), jnp.float32),
+            pltpu.VMEM((half, width), jnp.bfloat16),
+            pltpu.VMEM((half, width), jnp.bfloat16),
         ] + [dma] * 6,
         compiler_params=pltpu.CompilerParams(collective_id=0, has_side_effects=True, vmem_limit_bytes=GRANT),
-        name="replica_sum",
-    )(part)
+        name="swap_and_activate",
+    )(part, weight, bias[None, :])
+
+
+def flush_kernel(steps, act_ref, out_ref, sems):
+    size = act_ref.shape[0] // steps
+    spans = [pl.ds(i * size, size) for i in range(steps)]
+    copies = [pltpu.make_async_copy(act_ref.at[span], out_ref.at[span], sems.at[i]) for i, span in enumerate(spans)]
+    for copy in copies:
+        copy.start()
+    for copy in copies:
+        copy.wait()
+
+
+def flush(activations):
+    steps = largest_divisor(activations.shape[0] // 16, OUT_STEPS)
+    return pl.pallas_call(
+        functools.partial(flush_kernel, steps),
+        out_shape=jax.ShapeDtypeStruct(activations.shape, activations.dtype),
+        in_specs=[pl.BlockSpec(memory_space=pltpu.VMEM)],
+        out_specs=pl.BlockSpec(memory_space=pltpu.HBM),
+        scratch_shapes=[pltpu.SemaphoreType.DMA((steps,))],
+        compiler_params=pltpu.CompilerParams(vmem_limit_bytes=GRANT),
+        name="flush",
+    )(activations)
 
 
 def reduce_kernel(chips, chunks, part_ref, agg_ref, core_in, send_buf, recv_buf,
@@ -625,8 +669,9 @@
 def shards(blocks, replicas, features, weight, bias, tile_values, tile_place, tile_count):
     sources, held = gather_sources(features, tile_values, blocks, replicas)
     part = section_sums(sources, held, tile_place, tile_count)
-    aggregated = pair_sum(part) if replicas == 4 else replica_sum(part, replicas)
-    return activate(aggregated, weight, bias)
+    if replicas == 4:
+        return flush(swap_and_activate(part, weight, bias))
+    return activate(replica_sum(part, replicas), weight, bias)
 
 
 def solution(mesh):

time: 54.1 us -> 52.2 us (0.965)
  Pallas kernels: 53.9 us -> 51.6 us
    pallas_call x1, Pallas kernels: 3.66 us -> 1.88 us  [section_sums(): pl.pallas_call(functools.partial(sections_kernel, largest_divisor(slots,...]
where the time goes in v1:
time: 52.2 us; the launch traced here: 51.7 us
  Pallas kernels  51.6 us (99%)
    pallas_call x1, Pallas kernels, gather_sources(): pl.pallas_call(functools.partial(gather_kernel, blocks, replicas, section...  31.7 us
    pallas_call x1, Pallas kernels, swap_and_activate(): pl.pallas_call(functools.partial(swap_kernel, sizes), out_shape=jax.Shape...  16.7 us
    pallas_call x1, Pallas kernels, section_sums(): pl.pallas_call(functools.partial(sections_kernel, largest_divisor(slots,...  1.88 us
    pallas_call x1, Pallas kernels, flush(): pl.pallas_call(functools.partial(flush_kernel, steps), out_shape=jax.Shap...  1.38 us

profile of v1, /device:TPU:0, one launch (start us, length us, event | category | flops | bytes accessed | tf_op | source)
XLA Modules:
  0.0 51.7 jit_solution(18149353059849241687)
XLA Ops:
  0.0 0.0 copy-start.3
  0.0 0.0 copy-start.1
  0.0 31.7 %gather_sources.1 = (bf16[8,4096,128]{2,1,0:T(8,128)(2,1)S(1)}, bf16[1,2,160,128,128]{4,3,2,1,0:T(8,128)(2,1)S(1)}) custom-call(bf16[4096,128]{1,0:T(8,128)(2,1)} %features_ref.1, bf16[1,2,160,128,128]{4,3,2,1,0:T(8,128)(2,1)} %tiles_ref.1), custom_call_target="tpu_custom_call" | custom-call | bytes 100663296 | tf_op jit(solution)/shard_map/gather_sources/pallas_call | solution.py:372
  31.7 0.0 copy-done.3
  31.7 0.0 copy-done.1
  31.7 0.0 copy-start
  31.7 0.0 copy-start.2
  31.7 1.9 %section_sums.1.part_ref = f32[4096,128]{1,0:T(8,128)S(1)} custom-call(s32[1,2,160]{2,1,0:T(2,128)S(1)} %copy-done.1, s32[1,2]{1,0:T(1,128)S(1)} %copy-done.3, bf16[8,4096,128]{2,1,0:T(8,128)(2,1)S(1)} %get-tuple-element.7.source_ref, bf16[1,2,160,128,128]{4,3,2,1,0:T(8,128)(2,1)S(1)} %get-tuple-element.8.tiles_ref), custom_call_target="tpu_custom_call" | custom-call | tf_op jit(solution)/shard_map/section_sums/pallas_call | solution.py:424
  33.6 0.0 copy-done
  33.6 0.0 copy-done.2
  33.6 16.7 %swap_and_activate.1.act_ref = bf16[4096,256]{1,0:T(8,128)(2,1)S(1)} custom-call(f32[4096,128]{1,0:T(8,128)S(1)} %section_sums.1.part_ref, bf16[128,256]{1,0:T(8,128)(2,1)S(1)} %copy-done, f32[1,256]{1,0:T(1,128)S(1)} %bitcast.1), custom_call_target="tpu_custom_call" | custom-call | tf_op jit(solution)/shard_map/swap_and_activate/pallas_call | solution.py:499
  50.3 1.4 %flush.1 = bf16[4096,256]{1,0:T(8,128)(2,1)} custom-call(bf16[4096,256]{1,0:T(8,128)(2,1)S(1)} %swap_and_activate.1.act_ref), custom_call_target="tpu_custom_call" | custom-call | tf_op jit(solution)/shard_map/flush/pallas_call | solution.py:527
Async XLA Ops:
  0.0 31.7 %copy-start.3 = (s32[1,2]{1,0:T(1,128)S(1)}, s32[1,2]{1,0:T(1,128)}, u32[]{:S(2)}) copy-start(s32[1,2]{1,0:T(1,128)} %count_ref.1) | copy-start | bytes 28
  0.0 31.7 %copy-start.1 = (s32[1,2,160]{2,1,0:T(2,128)S(1)}, s32[1,2,160]{2,1,0:T(2,128)}, u32[]{:S(2)}) copy-start(s32[1,2,160]{2,1,0:T(2,128)} %place_ref.1) | copy-start | bytes 3844
  31.7 1.9 %copy-start = (bf16[128,256]{1,0:T(8,128)(2,1)S(1)}, bf16[128,256]{1,0:T(8,128)(2,1)}, u32[]{:S(2)}) copy-start(bf16[128,256]{1,0:T(8,128)(2,1)} %weight_ref.1) | copy-start | bytes 196612
  31.7 1.9 %copy-start.2 = (f32[256]{0:T(256)S(1)}, f32[256]{0:T(256)}, u32[]{:S(2)}) copy-start(f32[256]{0:T(256)} %param.8) | copy-start | bytes 3076

commit v2 on v1

--- a/solution.py
+++ b/solution.py
@@ -13,15 +13,16 @@
 GROUP = 80
 CHUNKS = 4
 PIECES = 16
-HOP = 6
-WAIT = 7
+HOP = 7
+WAIT = 5
 ROUNDS = 40
 LEAD = 0
 PASSES = 768
-SEED = 63485
+SEED = 36660
 EXPRESS = 1
-URGENCY = 0.1
+URGENCY = 0.2
 TOLL = 1.0
+SPREAD = 4.0
 OUT_STEPS = 8
 SWAPS = (1,) * 8
 GRANT = 16 * 1024 * 1024
@@ -64,7 +65,7 @@
     busy = {link: 0 for chip in chips for _, _, crossed in ways[chip] for link in crossed}
     load = dict.fromkeys(busy, 0)
     past = dict.fromkeys(busy, 0.0)
-    trees, best = {}, None
+    trees, best, mine = {}, None, {}
     keys = [(s, p) for p in range(pieces) for s in range(blocks)]
     turn, draw = list(keys), SEED
 
@@ -88,7 +89,7 @@
                     taken, toll = 0, 0.0
                     for link in crossed:
                         taken |= busy[link]
-                        toll += price[link]
+                        toll += price[link] + SPREAD * mine.get((s, link), 0) / pieces
                     taken >>= t
                     start = t + (~taken & (taken + 1)).bit_length() - 1
                     there = start + hop + len(crossed) - 1
@@ -106,6 +107,7 @@
                 for link in crossed:
                     busy[link] |= 1 << start
                     load[link] += 1
+                    mine[s, link] = mine.get((s, link), 0) + 1
                 tree.append((chip, way, start, other, crossed))
                 left.discard(other)
         return tree
@@ -116,6 +118,7 @@
                 for link in crossed:
                     busy[link] &= ~(1 << start)
                     load[link] -= 1
+                    mine[key[0], link] -= 1
             top = max(max(load.values()), 1)
             trees[key] = grow(key[0], {k: TOLL * (past[k] + (load[k] / top) ** 4) for k in load})
         last = {key: max(start for _, _, start, _, _ in tree) for key, tree in trees.items()}

time: 52.2 us -> 52 us (level)
    pallas_call x1, Pallas kernels: 31.7 us -> 30.4 us  [gather_sources(): pl.pallas_call(functools.partial(gather_kernel, blocks, replicas, section...]
    pallas_call x1, Pallas kernels: 1.88 us -> 2.7 us  [section_sums(): pl.pallas_call(functools.partial(sections_kernel, largest_divisor(slots,...]
where the time goes in v2:
time: 52 us; the launch traced here: 51.6 us
  Pallas kernels  51.5 us (99%)
    pallas_call x1, Pallas kernels, gather_sources(): pl.pallas_call(functools.partial(gather_kernel, blocks, replicas, section...  30.4 us
    pallas_call x1, Pallas kernels, swap_and_activate(): pl.pallas_call(functools.partial(swap_kernel, sizes), out_shape=jax.Shape...  17.1 us
    pallas_call x1, Pallas kernels, section_sums(): pl.pallas_call(functools.partial(sections_kernel, largest_divisor(slots,...  2.7 us
    pallas_call x1, Pallas kernels, flush(): pl.pallas_call(functools.partial(flush_kernel, steps), out_shape=jax.Shap...  1.38 us

profile of v2, /device:TPU:0, one launch (start us, length us, event | category | flops | bytes accessed | tf_op | source)
XLA Modules:
  0.0 51.6 jit_solution(10617150116488200649)
XLA Ops:
  0.0 0.0 copy-start.3
  0.0 0.0 copy-start.1
  0.0 30.4 %gather_sources.1 = (bf16[8,4096,128]{2,1,0:T(8,128)(2,1)S(1)}, bf16[1,2,160,128,128]{4,3,2,1,0:T(8,128)(2,1)S(1)}) custom-call(bf16[4096,128]{1,0:T(8,128)(2,1)} %features_ref.1, bf16[1,2,160,128,128]{4,3,2,1,0:T(8,128)(2,1)} %tiles_ref.1), custom_call_target="tpu_custom_call" | custom-call | bytes 100663296 | tf_op jit(solution)/shard_map/gather_sources/pallas_call | solution.py:375
  30.4 0.0 copy-done.3
  30.4 0.0 copy-done.1
  30.4 0.0 copy-start
  30.4 0.0 copy-start.2
  30.4 2.7 %section_sums.1.part_ref = f32[4096,128]{1,0:T(8,128)S(1)} custom-call(s32[1,2,160]{2,1,0:T(2,128)S(1)} %copy-done.1, s32[1,2]{1,0:T(1,128)S(1)} %copy-done.3, bf16[8,4096,128]{2,1,0:T(8,128)(2,1)S(1)} %get-tuple-element.7.source_ref, bf16[1,2,160,128,128]{4,3,2,1,0:T(8,128)(2,1)S(1)} %get-tuple-element.8.tiles_ref), custom_call_target="tpu_custom_call" | custom-call | tf_op jit(solution)/shard_map/section_sums/pallas_call | solution.py:427
  33.1 0.0 copy-done
  33.1 0.0 copy-done.2
  33.1 17.1 %swap_and_activate.1.act_ref = bf16[4096,256]{1,0:T(8,128)(2,1)S(1)} custom-call(f32[4096,128]{1,0:T(8,128)S(1)} %section_sums.1.part_ref, bf16[128,256]{1,0:T(8,128)(2,1)S(1)} %copy-done, f32[1,256]{1,0:T(1,128)S(1)} %bitcast.1), custom_call_target="tpu_custom_call" | custom-call | tf_op jit(solution)/shard_map/swap_and_activate/pallas_call | solution.py:502
  50.3 1.4 %flush.1 = bf16[4096,256]{1,0:T(8,128)(2,1)} custom-call(bf16[4096,256]{1,0:T(8,128)(2,1)S(1)} %swap_and_activate.1.act_ref), custom_call_target="tpu_custom_call" | custom-call | tf_op jit(solution)/shard_map/flush/pallas_call | solution.py:530
Async XLA Ops:
  0.0 30.4 %copy-start.3 = (s32[1,2]{1,0:T(1,128)S(1)}, s32[1,2]{1,0:T(1,128)}, u32[]{:S(2)}) copy-start(s32[1,2]{1,0:T(1,128)} %count_ref.1) | copy-start | bytes 28
  0.0 30.4 %copy-start.1 = (s32[1,2,160]{2,1,0:T(2,128)S(1)}, s32[1,2,160]{2,1,0:T(2,128)}, u32[]{:S(2)}) copy-start(s32[1,2,160]{2,1,0:T(2,128)} %place_ref.1) | copy-start | bytes 3844
  30.4 2.7 %copy-start = (bf16[128,256]{1,0:T(8,128)(2,1)S(1)}, bf16[128,256]{1,0:T(8,128)(2,1)}, u32[]{:S(2)}) copy-start(bf16[128,256]{1,0:T(8,128)(2,1)} %weight_ref.1) | copy-start | bytes 196612
  30.4 2.7 %copy-start.2 = (f32[256]{0:T(256)S(1)}, f32[256]{0:T(256)}, u32[]{:S(2)}) copy-start(f32[256]{0:T(256)} %param.8) | copy-start | bytes 3076

commit v3 on v2

--- a/solution.py
+++ b/solution.py
@@ -13,17 +13,17 @@
 GROUP = 80
 CHUNKS = 4
 PIECES = 16
-HOP = 7
+HOP = 8
 WAIT = 5
 ROUNDS = 40
 LEAD = 0
 PASSES = 768
-SEED = 36660
+SEED = 70599
 EXPRESS = 1
-URGENCY = 0.2
+URGENCY = 0.25
 TOLL = 1.0
-SPREAD = 4.0
-OUT_STEPS = 8
+SPREAD = 6.0
+OUT_STEPS = 2
 SWAPS = (1,) * 8
 GRANT = 16 * 1024 * 1024
 

time: 52 us -> 51.9 us (level)
    pallas_call x1, Pallas kernels: 2.7 us -> 3.26 us  [section_sums(): pl.pallas_call(functools.partial(sections_kernel, largest_divisor(slots,...]
where the time goes in v3:
time: 51.9 us
  Pallas kernels  51.8 us (100%)
    pallas_call x1, Pallas kernels, gather_sources(): pl.pallas_call(functools.partial(gather_kernel, blocks, replicas, section...  30.3 us
    pallas_call x1, Pallas kernels, swap_and_activate(): pl.pallas_call(functools.partial(swap_kernel, sizes), out_shape=jax.Shape...  16.9 us
    pallas_call x1, Pallas kernels, section_sums(): pl.pallas_call(functools.partial(sections_kernel, largest_divisor(slots,...  3.26 us
    pallas_call x1, Pallas kernels, flush(): pl.pallas_call(functools.partial(flush_kernel, steps), out_shape=jax.Shap...  1.34 us

profile of v3, /device:TPU:0, one launch (start us, length us, event | category | flops | bytes accessed | tf_op | source)
XLA Modules:
  0.0 51.9 jit_solution(10985928800538320192)
XLA Ops:
  0.0 0.0 copy-start.3
  0.0 0.0 copy-start.1
  0.0 30.3 %gather_sources.1 = (bf16[8,4096,128]{2,1,0:T(8,128)(2,1)S(1)}, bf16[1,2,160,128,128]{4,3,2,1,0:T(8,128)(2,1)S(1)}) custom-call(bf16[4096,128]{1,0:T(8,128)(2,1)} %features_ref.1, bf16[1,2,160,128,128]{4,3,2,1,0:T(8,128)(2,1)} %tiles_ref.1), custom_call_target="tpu_custom_call" | custom-call | bytes 100663296 | tf_op jit(solution)/shard_map/gather_sources/pallas_call | solution.py:375
  30.3 0.0 copy-done.3
  30.3 0.0 copy-done.1
  30.3 0.0 copy-start
  30.4 0.0 copy-start.2
  30.4 3.3 %section_sums.1.part_ref = f32[4096,128]{1,0:T(8,128)S(1)} custom-call(s32[1,2,160]{2,1,0:T(2,128)S(1)} %copy-done.1, s32[1,2]{1,0:T(1,128)S(1)} %copy-done.3, bf16[8,4096,128]{2,1,0:T(8,128)(2,1)S(1)} %get-tuple-element.7.source_ref, bf16[1,2,160,128,128]{4,3,2,1,0:T(8,128)(2,1)S(1)} %get-tuple-element.8.tiles_ref), custom_call_target="tpu_custom_call" | custom-call | tf_op jit(solution)/shard_map/section_sums/pallas_call | solution.py:427
  33.6 0.0 copy-done
  33.6 0.0 copy-done.2
  33.7 16.9 %swap_and_activate.1.act_ref = bf16[4096,256]{1,0:T(8,128)(2,1)S(1)} custom-call(f32[4096,128]{1,0:T(8,128)S(1)} %section_sums.1.part_ref, bf16[128,256]{1,0:T(8,128)(2,1)S(1)} %copy-done, f32[1,256]{1,0:T(1,128)S(1)} %bitcast.1), custom_call_target="tpu_custom_call" | custom-call | tf_op jit(solution)/shard_map/swap_and_activate/pallas_call | solution.py:502
  50.5 1.3 %flush.1 = bf16[4096,256]{1,0:T(8,128)(2,1)} custom-call(bf16[4096,256]{1,0:T(8,128)(2,1)S(1)} %swap_and_activate.1.act_ref), custom_call_target="tpu_custom_call" | custom-call | tf_op jit(solution)/shard_map/flush/pallas_call | solution.py:530
Async XLA Ops:
  0.0 30.3 %copy-start.3 = (s32[1,2]{1,0:T(1,128)S(1)}, s32[1,2]{1,0:T(1,128)}, u32[]{:S(2)}) copy-start(s32[1,2]{1,0:T(1,128)} %count_ref.1) | copy-start | bytes 28
  0.0 30.3 %copy-start.1 = (s32[1,2,160]{2,1,0:T(2,128)S(1)}, s32[1,2,160]{2,1,0:T(2,128)}, u32[]{:S(2)}) copy-start(s32[1,2,160]{2,1,0:T(2,128)} %place_ref.1) | copy-start | bytes 3844
  30.3 3.3 %copy-start = (bf16[128,256]{1,0:T(8,128)(2,1)S(1)}, bf16[128,256]{1,0:T(8,128)(2,1)}, u32[]{:S(2)}) copy-start(bf16[128,256]{1,0:T(8,128)(2,1)} %weight_ref.1) | copy-start | bytes 196612
  30.4 3.3 %copy-start.2 = (f32[256]{0:T(256)S(1)}, f32[256]{0:T(256)}, u32[]{:S(2)}) copy-start(f32[256]{0:T(256)} %param.8) | copy-start | bytes 3076

commit v4 on v2

--- a/solution.py
+++ b/solution.py
@@ -346,7 +346,7 @@
         return carry
 
     lax.fori_loop(0, steps, step, 0)
-    lax.fori_loop(0, steps * 3 // 4, drain, 0)
+    lax.fori_loop(0, steps, drain, 0)
     for n, (i, first) in enumerate(words):
         source = lax.rem(blk - rep * sections - i + blocks, blocks)
         mask = table_ref[steps + n]
@@ -356,7 +356,6 @@
             return carry
 
         lax.fori_loop(0, run, leaf, 0)
-    lax.fori_loop(steps * 3 // 4, steps, drain, 0)
     held.wait()
 
 

time: 52 us -> 51.7 us (level)
  no operation moved by 1% of the time
where the time goes in v4:
time: 51.7 us; the launch traced here: 51.4 us
  Pallas kernels  51.3 us (99%)
    pallas_call x1, Pallas kernels, gather_sources(): pl.pallas_call(functools.partial(gather_kernel, blocks, replicas, section...  30.4 us
    pallas_call x1, Pallas kernels, swap_and_activate(): pl.pallas_call(functools.partial(swap_kernel, sizes), out_shape=jax.Shape...  16.9 us
    pallas_call x1, Pallas kernels, section_sums(): pl.pallas_call(functools.partial(sections_kernel, largest_divisor(slots,...  2.7 us
    pallas_call x1, Pallas kernels, flush(): pl.pallas_call(functools.partial(flush_kernel, steps), out_shape=jax.Shap...  1.38 us

profile of v4, /device:TPU:0, one launch (start us, length us, event | category | flops | bytes accessed | tf_op | source)
XLA Modules:
  0.0 51.4 jit_solution(12377643281357240061)
XLA Ops:
  0.0 0.0 copy-start.3
  0.0 0.0 copy-start.1
  0.0 30.4 %gather_sources.1 = (bf16[8,4096,128]{2,1,0:T(8,128)(2,1)S(1)}, bf16[1,2,160,128,128]{4,3,2,1,0:T(8,128)(2,1)S(1)}) custom-call(bf16[4096,128]{1,0:T(8,128)(2,1)} %features_ref.1, bf16[1,2,160,128,128]{4,3,2,1,0:T(8,128)(2,1)} %tiles_ref.1), custom_call_target="tpu_custom_call" | custom-call | bytes 100663296 | tf_op jit(solution)/shard_map/gather_sources/pallas_call | solution.py:374
  30.4 0.0 copy-done.3
  30.4 0.0 copy-done.1
  30.4 0.0 copy-start
  30.4 0.0 copy-start.2
  30.4 2.7 %section_sums.1.part_ref = f32[4096,128]{1,0:T(8,128)S(1)} custom-call(s32[1,2,160]{2,1,0:T(2,128)S(1)} %copy-done.1, s32[1,2]{1,0:T(1,128)S(1)} %copy-done.3, bf16[8,4096,128]{2,1,0:T(8,128)(2,1)S(1)} %get-tuple-element.7.source_ref, bf16[1,2,160,128,128]{4,3,2,1,0:T(8,128)(2,1)S(1)} %get-tuple-element.8.tiles_ref), custom_call_target="tpu_custom_call" | custom-call | tf_op jit(solution)/shard_map/section_sums/pallas_call | solution.py:426
  33.1 0.0 copy-done
  33.1 0.0 copy-done.2
  33.1 16.9 %swap_and_activate.1.act_ref = bf16[4096,256]{1,0:T(8,128)(2,1)S(1)} custom-call(f32[4096,128]{1,0:T(8,128)S(1)} %section_sums.1.part_ref, bf16[128,256]{1,0:T(8,128)(2,1)S(1)} %copy-done, f32[1,256]{1,0:T(1,128)S(1)} %bitcast.1), custom_call_target="tpu_custom_call" | custom-call | tf_op jit(solution)/shard_map/swap_and_activate/pallas_call | solution.py:501
  50.1 1.4 %flush.1 = bf16[4096,256]{1,0:T(8,128)(2,1)} custom-call(bf16[4096,256]{1,0:T(8,128)(2,1)S(1)} %swap_and_activate.1.act_ref), custom_call_target="tpu_custom_call" | custom-call | tf_op jit(solution)/shard_map/flush/pallas_call | solution.py:529
Async XLA Ops:
  0.0 30.4 %copy-start.3 = (s32[1,2]{1,0:T(1,128)S(1)}, s32[1,2]{1,0:T(1,128)}, u32[]{:S(2)}) copy-start(s32[1,2]{1,0:T(1,128)} %count_ref.1) | copy-start | bytes 28
  0.0 30.4 %copy-start.1 = (s32[1,2,160]{2,1,0:T(2,128)S(1)}, s32[1,2,160]{2,1,0:T(2,128)}, u32[]{:S(2)}) copy-start(s32[1,2,160]{2,1,0:T(2,128)} %place_ref.1) | copy-start | bytes 3844
  30.4 2.7 %copy-start = (bf16[128,256]{1,0:T(8,128)(2,1)S(1)}, bf16[128,256]{1,0:T(8,128)(2,1)}, u32[]{:S(2)}) copy-start(bf16[128,256]{1,0:T(8,128)(2,1)} %weight_ref.1) | copy-start | bytes 196612
  30.4 2.7 %copy-start.2 = (f32[256]{0:T(256)S(1)}, f32[256]{0:T(256)}, u32[]{:S(2)}) copy-start(f32[256]{0:T(256)} %param.8) | copy-start | bytes 3076
